TPU v7x, 32 devices: a whole 2x2x4 slice. The times are simulated.
32 devices in a mesh: men: 16 (over z, x, core), women: 2 (over y).
Axes of the slice: x: 2, y: 2, z: 4, core: 2. Of those that a mesh axis runs over, the one named last changes fastest.
Arguments:
- men_traits: bfloat16 [64, 16384], P(None, ('men', 'women')), may hold values from -4 to 4
- women_traits: bfloat16 [64, 8192], P(None, ('women', 'men')), may hold values from -4 to 4
- affinity: float32 [64, 64], replicated, may hold values from -0.375 to 0.375
- observed: float32 [64, 64], replicated, may hold values from -0.25 to 0.25
- men_mass: float32 [16384], P('men'), may hold values from 0.5 to 2
- women_mass: float32 [8192], P('women'), may hold values from 0.5 to 2
Outputs:
- men_scale: float32 [16384], P('men')
- women_scale: float32 [8192], P('women')
- updated: float32 [64, 64], replicated
All inputs are finite; a program needn't handle non-finite values.
Results may differ from a plain program's by a relative error of at most 0.0022.
Values may be sent and summed in bfloat16 or wider, within the bound.
A program may use at most 64 MiB of HBM per device.

v0:
```python
import functools
import math
import jax
import jax.numpy as jnp
from jax import lax
from jax.experimental import pallas as pl
from jax.experimental.pallas import tpu as pltpu
from jax.sharding import PartitionSpec as P

F32, BF16 = jnp.float32, jnp.bfloat16
MESH = pl.DeviceIdType.MESH
LHS_T = (((0,), (0,)), ((), ()))
RHS_T = (((1,), (1,)), ((), ()))


def split3(value):
    high = value.astype(BF16)
    rest = value - high.astype(F32)
    mid = rest.astype(BF16)
    low = (rest - mid.astype(F32)).astype(BF16)
    return high, mid, low


def factors(men):
    cores = 2 if men % 2 == 0 else 1
    chips = men // cores
    planes = 1 << (chips.bit_length() // 2)
    if chips % planes:
        planes = 1
    return planes, chips // planes, cores


def body(dims, women_axis, men_total, women_total,
         men_ref, women_ref, aff_ref, obs_ref, mm_ref, wm_ref,
         ms_out, ws_out, up_out,
         men_buf, wom_buf, scaled_ref, e_ref, t_ref, col_ref, r_buf, a_buf, z_buf,
         my_buf, ma_buf, mz_buf,
         own_sem, gy_s, gy_r, gz_s, gz_r, gx_s, gx_r, gc_s, gc_r,
         ry_s, ry_r, ca_s, ca_r, cz_s, cz_r):
    zs, xs, cs = dims
    ws = women_axis
    n = zs * xs * cs
    traits, wb = women_ref.shape
    rows = mm_ref.shape[1]
    log_count = math.log(women_total)
    mi = lax.axis_index("men")
    yi = lax.axis_index("women")
    ci = lax.rem(mi, cs)
    xi = lax.rem(lax.div(mi, cs), xs)
    zi = lax.div(mi, cs * xs)

    def men_at(z, x, c):
        return (z * xs + x) * cs + c

    def plus(value, step, size):
        return lax.rem(value + step, size)

    plane = [(dc, dx) for dc in range(cs) for dx in range(xs) if (dc, dx) != (0, 0)]
    plane_ids = [(men_at(zi, plus(xi, dx, xs), plus(ci, dc, cs)), yi) for dc, dx in plane]
    z_ids = [(men_at(plus(zi, dz, zs), xi, ci), yi) for dz in range(1, zs)]
    y_ids = [(mi, plus(yi, dy, ws)) for dy in range(1, ws)]

    own = pltpu.make_async_copy(women_ref, wom_buf.at[ci, xi, zi], own_sem)
    own.start()
    barrier = pltpu.get_barrier_semaphore()
    everyone = plane_ids + z_ids + y_ids
    for peer in everyone:
        pl.semaphore_signal(barrier, inc=1, device_id=peer, device_id_type=MESH)
    pl.semaphore_wait(barrier, len(everyone))

    def remote(src, dst, send, recv, peer):
        return pltpu.make_async_remote_copy(
            src_ref=src, dst_ref=dst, send_sem=send, recv_sem=recv,
            device_id=peer, device_id_type=MESH)

    def z_copy(dz):
        return remote(women_ref, wom_buf.at[ci, xi, zi], gz_s.at[dz], gz_r.at[dz],
                      (men_at(plus(zi, dz, zs), xi, ci), yi))

    def block_of(dx, dz):
        return wom_buf.at[ci, plus(xi, xs - dx, xs), plus(zi, zs - dz, zs)]

    def x_copy(dx, dz):
        held = block_of(0, dz)
        return remote(held, held, gx_s.at[dx, dz], gx_r.at[dx, dz],
                      (men_at(zi, plus(xi, dx, xs), ci), yi))

    def c_copy(dx, dz):
        held = block_of(dx, dz)
        return remote(held, held, gc_s.at[dx, dz], gc_r.at[dx, dz],
                      (men_at(zi, xi, plus(ci, 1, cs)), yi))

    def forward(dz):
        for dx in range(1, xs):
            x_copy(dx, dz).start()
        if cs > 1:
            c_copy(0, dz).start()

    men_copies = []
    for dy, peer in enumerate(y_ids):
        copy = remote(men_ref, men_buf.at[yi], gy_s.at[dy], gy_r.at[dy], peer)
        copy.start()
        men_copies.append(copy)
    for dz in range(1, zs):
        z_copy(dz).start()
    own.wait()
    forward(0)
    men_buf[yi] = men_ref[...]
    for copy in men_copies:
        copy.wait_recv()

    men_full = jnp.concatenate([men_buf[y] for y in range(ws)], axis=1)
    high, mid, low = [
        lax.dot_general(men_full, part, LHS_T, preferred_element_type=F32)
        for part in split3(aff_ref[...])
    ]
    scaled_ref[...] = ((low + mid) + high).astype(BF16)
    ones = jnp.ones((16, wb), BF16)
    tile = math.gcd(rows, 256)

    def fill(t, total):
        dz = lax.rem(t, zs)
        dx = lax.rem(lax.div(t, zs), xs)
        dc = lax.div(t, zs * xs)

        @pl.when((t > 0) & (t < zs))
        def _():
            z_copy(dz).wait_recv()
            forward(dz)

        if xs > 1:
            @pl.when((t >= zs) & (t < zs * xs))
            def _():
                x_copy(dx, dz).wait_recv()
                if cs > 1:
                    c_copy(dx, dz).start()

        if cs > 1:
            @pl.when(t >= zs * xs)
            def _():
                c_copy(dx, dz).wait_recv()

        bc = plus(ci, dc, cs)
        bx = plus(xi, xs - dx, xs)
        bz = plus(zi, zs - dz, zs)
        q = (bc * xs + bx) * zs + bz
        block = wom_buf[bc, bx, bz]
        for start in range(0, rows, tile):
            surplus = jnp.dot(scaled_ref[start:start + tile, :], block, preferred_element_type=F32)
            e_ref[q, start:start + tile, :] = jnp.exp(surplus - log_count).astype(BF16)
        return total + lax.dot_general(ones, e_ref[q], RHS_T, preferred_element_type=F32)

    pending = []

    def group_sum(value, buf, me, send, recv, peers):
        if not peers:
            return value
        buf[me] = value
        copies = []
        for k, peer in enumerate(peers):
            copy = remote(buf.at[me], buf.at[me], send.at[k], recv.at[k], peer)
            copy.start()
            copies.append(copy)
        for copy in copies:
            copy.wait_recv()
        pending.extend(copies)
        total = buf[0]
        for slot in range(1, buf.shape[0]):
            total = total + buf[slot]
        return total

    def men_update(it, row_sum):
        total = group_sum(row_sum, r_buf.at[it], yi, ry_s.at[it], ry_r.at[it], y_ids)
        return mm_ref[...] / total

    order = [((z * xs + x) * cs + c) for c in range(cs) for x in range(xs) for z in range(zs)]
    mass_q = jnp.concatenate([wm_ref[:, p * wb:(p + 1) * wb] for p in order], axis=0)
    plane_me = ci * xs + xi

    def women_update(it, partial):
        total = group_sum(partial, a_buf.at[it], plane_me, ca_s.at[it], ca_r.at[it], plane_ids)
        total = group_sum(total, z_buf.at[it], zi, cz_s.at[it], cz_r.at[it], z_ids)
        return mass_q / total

    zeros13 = jnp.zeros((13, rows), BF16)
    zeros13w = jnp.zeros((13, wb), BF16)

    total = lax.fori_loop(0, n, fill, jnp.zeros((16, rows), F32))
    scale = men_update(0, total[0:1, :])

    def sweep(step, carry):
        if n <= 16:
            for q in range(n):
                carry = step(q, carry)
            return carry
        return lax.fori_loop(0, n, step, carry)

    left0 = jnp.concatenate(list(split3(scale)) + [zeros13], axis=0)

    def col_step(q, carry):
        out = jnp.dot(left0, e_ref[q], preferred_element_type=F32)
        col_ref[pl.ds(q, 1), :] = out[0:1] + out[1:2] + out[2:3]
        return carry

    sweep(col_step, 0)
    col_ref[...] = women_update(0, col_ref[...])

    def row_step(q, total):
        lines = jnp.concatenate(list(split3(col_ref[pl.ds(q, 1), :])) + [zeros13w], axis=0)
        return total + lax.dot_general(lines, e_ref[q], RHS_T, preferred_element_type=F32)

    total = sweep(row_step, jnp.zeros((16, rows), F32))
    scale = men_update(1, total[0:1] + total[1:2] + total[2:3])
    ms_out[...] = scale

    weighted = (men_full.astype(F32) * scale).astype(BF16)
    left = jnp.concatenate([weighted] + list(split3(scale)) + [zeros13], axis=0)

    def both_step(q, carry):
        out = jnp.dot(left, e_ref[q], preferred_element_type=F32)
        t_ref[q] = out[0:traits]
        col_ref[pl.ds(q, 1), :] = (out[traits:traits + 1] + out[traits + 1:traits + 2]
                                   + out[traits + 2:traits + 3])
        return carry

    sweep(both_step, 0)
    women_scale = women_update(1, col_ref[...])
    col_ref[...] = women_scale
    for q, p in enumerate(order):
        ws_out[:, p * wb:(p + 1) * wb] = women_scale[q:q + 1, :]

    def moment_step(q, moment):
        c, x, z = q // (xs * zs), (q // zs) % xs, q % zs
        inner = t_ref[q] * col_ref[pl.ds(q, 1), :]
        high = inner.astype(BF16)
        low = (inner - high.astype(F32)).astype(BF16)
        both = jnp.concatenate([high, low], axis=0)
        return moment + lax.dot_general(both, wom_buf[c, x, z], RHS_T, preferred_element_type=F32)

    moment = sweep(moment_step, jnp.zeros((2 * traits, traits), F32))
    moment = moment[0:traits] + moment[traits:]
    half = traits // 2
    packed = jnp.concatenate([moment[0:half], moment[half:]], axis=1)
    packed = group_sum(packed, my_buf, yi, ry_s.at[2], ry_r.at[2], y_ids)
    packed = group_sum(packed, ma_buf, plane_me, ca_s.at[2], ca_r.at[2], plane_ids)
    packed = group_sum(packed, mz_buf, zi, cz_s.at[2], cz_r.at[2], z_ids)
    moment = jnp.concatenate([packed[:, 0:traits], packed[:, traits:]], axis=0)
    up_out[...] = aff_ref[...] + obs_ref[...] - moment * (1.0 / men_total)

    for copy in men_copies + pending:
        copy.wait_send()
    for dz in range(1, zs):
        z_copy(dz).wait_send()
    for dz in range(zs):
        for dx in range(1, xs):
            x_copy(dx, dz).wait_send()
        if cs > 1:
            for dx in range(xs):
                c_copy(dx, dz).wait_send()


def solution(mesh):
    men_axis, women_axis = mesh.shape["men"], mesh.shape["women"]
    dims = factors(men_axis)
    zs, xs, cs = dims

    def on_device(men_traits, women_traits, affinity, observed, men_mass, women_mass):
        traits, mb = men_traits.shape
        wb = women_traits.shape[1]
        rows, cols = men_mass.shape[0], women_mass.shape[0]
        n, group = men_axis, xs * cs
        dma = pltpu.SemaphoreType.DMA
        vmem = pl.BlockSpec(memory_space=pltpu.VMEM)
        half = traits // 2

        def at_least(k):
            return max(k, 1)

        out = pl.pallas_call(
            functools.partial(body, dims, women_axis, rows * men_axis, cols * women_axis),
            out_shape=(
                jax.ShapeDtypeStruct((1, rows), F32),
                jax.ShapeDtypeStruct((1, cols), F32),
                jax.ShapeDtypeStruct((traits, traits), F32),
            ),
            in_specs=[vmem] * 6,
            out_specs=(vmem, vmem, vmem),
            scratch_shapes=[
                pltpu.VMEM((women_axis, traits, mb), BF16),
                pltpu.VMEM((cs, xs, zs, traits, wb), BF16),
                pltpu.VMEM((rows, traits), BF16),
                pltpu.VMEM((n, rows, wb), BF16),
                pltpu.VMEM((n, traits, wb), F32),
                pltpu.VMEM((n, wb), F32),
                pltpu.VMEM((2, women_axis, 1, rows), F32),
                pltpu.VMEM((2, group, n, wb), F32),
                pltpu.VMEM((2, zs, n, wb), F32),
                pltpu.VMEM((women_axis, half, 2 * traits), F32),
                pltpu.VMEM((group, half, 2 * traits), F32),
                pltpu.VMEM((zs, half, 2 * traits), F32),
                dma(()),
                dma((women_axis,)), dma((women_axis,)),
                dma((zs,)), dma((zs,)),
                dma((xs, zs)), dma((xs, zs)),
                dma((xs, zs)), dma((xs, zs)),
                dma((3, women_axis)), dma((3, women_axis)),
                dma((3, group)), dma((3, group)),
                dma((3, zs)), dma((3, zs)),
            ],
            compiler_params=pltpu.CompilerParams(
                collective_id=0, has_side_effects=True, vmem_limit_bytes=60 * 1024 * 1024),
        )(men_traits, women_traits, affinity, observed,
          men_mass.reshape(1, rows), women_mass.reshape(1, cols))
        return out[0].reshape(rows), out[1].reshape(cols), out[2]

    placed = (P(None, ("men", "women")), P(None, ("women", "men")), P(), P(), P("men"), P("women"))
    return jax.shard_map(
        on_device,
        mesh=mesh,
        in_specs=placed,
        out_specs=(P("men"), P("women"), P()),
        check_vma=False,
    )
```

profile of v0, /device:TPU:0, one launch (start us, length us, event | category | flops | bytes accessed | tf_op | source)
XLA Modules:
  0.0 57.1 jit_solution(8834380048031340742)
XLA Ops:
  0.6 53.3 %shard_map.85 = (f32[1,1024]{1,0:T(1,128)}, f32[1,4096]{1,0:T(1,128)}, f32[64,64]{1,0:T(8,128)}) custom-call(bf16[64,512]{1,0:T(8,128)(2,1)} %men_ref.1, bf16[64,256]{1,0:T(8,128)(2,1)} %women_ref.1, f32[64,64]{1,0:T(8,128)} %aff_ref.1, f32[64,64]{1,0:T(8,128)} %obs_ref.1, f32[1,1024]{1,0:T(1,128)} %bitcast.6, f32[1,4096]{1,0:T(1,128)} %bitcast.4), custom_call_target="tpu_custom_call" | custom-call | tf_op jit(solution)/shard_map/pallas_call | solution.py:279
  53.9 0.0 copy-start
  53.9 1.3 %copy.12 = f32[1024]{0:T(1024)} copy(f32[1024]{0:T(1024)} %bitcast.7) | data formatting | bytes 8192
  55.2 1.3 %copy.13 = f32[4096]{0:T(1024)} copy(f32[4096]{0:T(1024)} %bitcast.5) | data formatting | bytes 32768
  56.5 0.0 copy-done
  56.5 0.6 %copy.14 = f32[64,64]{1,0:T(8,128)} copy(f32[64,64]{1,0:T(8,128)S(1)} %copy-done) | data formatting | bytes 32768
Async XLA Ops:
  53.9 2.6 %copy-start = (f32[64,64]{1,0:T(8,128)S(1)}, f32[64,64]{1,0:T(8,128)}, u32[]{:S(2)}) copy-start(f32[64,64]{1,0:T(8,128)} %get-tuple-element.14) | copy-start | bytes 49156
where the time goes:
time: 57.5 us; the launch traced here: 57.1 us
  Pallas kernels  53.3 us (93%)
  local copies, waits for them, and re-layouts  3.22 us (6%)
  between operations  0.65 us (1%)
    pallas_call x1, Pallas kernels, on_device(): pl.pallas_call(functools.partial(body, dims, women_axis, rows * men_axis,...  53.3 us
    unnamed x5, local copies, waits for them, and re-layouts  3.22 us

commit v1 on v0

v1 whole, which is shorter than its diff:
```python
import functools
import math
import jax
import jax.numpy as jnp
from jax import lax
from jax.experimental import pallas as pl
from jax.experimental.pallas import tpu as pltpu
from jax.sharding import PartitionSpec as P

F32, BF16 = jnp.float32, jnp.bfloat16
MESH = pl.DeviceIdType.MESH
LHS_T = (((0,), (0,)), ((), ()))
RHS_T = (((1,), (1,)), ((), ()))


def split3(value):
    high = value.astype(BF16)
    rest = value - high.astype(F32)
    mid = rest.astype(BF16)
    low = (rest - mid.astype(F32)).astype(BF16)
    return high, mid, low


def factors(men):
    cores = 2 if men % 2 == 0 else 1
    chips = men // cores
    planes = 1 << (chips.bit_length() // 2)
    if chips % planes:
        planes = 1
    return planes, chips // planes, cores


def body(dims, ws, men_total, women_total,
         men_ref, women_ref, aff_hbm, obs_hbm, mm_hbm, wm_hbm,
         ms_out, ws_out, up_out,
         men_buf, wom_buf, scaled_ref, e_ref, t_ref, col_ref, rsum_ref, scale_ref,
         aff_ref, obs_ref, wm_ref, mass_buf, wx_buf,
         r_buf, c_buf, mxy_buf, mc_buf, mz_buf,
         own_sem, gm_s, gm_r, gz_s, gz_r, gc_s, gc_r, mm_s, mm_r, wx_s, wx_r,
         rx_s, rx_r, cz_s, cz_r, mc_s, mc_r, mz_s, mz_r):
    zs, xs, cs = dims
    nm, nb = xs * ws, zs * cs
    traits, wb = women_ref.shape
    mb = men_ref.shape[1]
    rows = mm_hbm.shape[1]
    group_rows = nm * mb
    log_count = math.log(women_total)
    mi = lax.axis_index("men")
    yi = lax.axis_index("women")
    ci = lax.rem(mi, cs)
    xi = lax.rem(lax.div(mi, cs), xs)
    zi = lax.div(mi, cs * xs)
    xy_me = xi * ws + yi
    zc_me = ci * zs + zi

    def plus(value, step, size):
        return lax.rem(value + step, size)

    def xy_peer(dx, dy):
        return ((zi * xs + plus(xi, dx, xs)) * cs + ci, plus(yi, dy, ws))

    def zc_peer(dc, dz):
        return ((plus(zi, dz, zs) * xs + xi) * cs + plus(ci, dc, cs), yi)

    xy_ids = [xy_peer(dx, dy) for dx in range(xs) for dy in range(ws) if dx + dy]
    zc_ids = [zc_peer(dc, dz) for dc in range(cs) for dz in range(zs) if dc + dz]
    x_ids = [xy_peer(dx, 0) for dx in range(1, xs)]
    c_ids = [zc_peer(dc, 0) for dc in range(1, cs)]
    z_ids = [zc_peer(0, dz) for dz in range(1, zs)]

    barrier = pltpu.get_barrier_semaphore()
    everyone = xy_ids + zc_ids
    for peer in everyone:
        pl.semaphore_signal(barrier, inc=1, device_id=peer, device_id_type=MESH)
    local = [
        pltpu.make_async_copy(src, dst, own_sem.at[k])
        for k, (src, dst) in enumerate([
            (men_ref, men_buf.at[xy_me]), (women_ref, wom_buf.at[zc_me]), (aff_hbm, aff_ref),
            (mm_hbm, mass_buf.at[xi]), (wm_hbm, wm_ref), (obs_hbm, obs_ref)])
    ]
    for copy in local:
        copy.start()
    pl.semaphore_wait(barrier, len(everyone))

    def remote(src, dst, send, recv, peer):
        return pltpu.make_async_remote_copy(
            src_ref=src, dst_ref=dst, send_sem=send, recv_sem=recv,
            device_id=peer, device_id_type=MESH)

    def z_copy(dz):
        return remote(women_ref, wom_buf.at[zc_me], gz_s.at[dz], gz_r.at[dz], zc_peer(0, dz))

    def c_copy(dz):
        held = wom_buf.at[ci * zs + plus(zi, zs - dz, zs)]
        return remote(held, held, gc_s.at[dz], gc_r.at[dz], zc_peer(1, 0))

    def m_copy(k):
        return remote(men_ref, men_buf.at[xy_me], gm_s.at[k], gm_r.at[k],
                      xy_peer(lax.div(k, ws), lax.rem(k, ws)))

    for dz in range(1, zs):
        z_copy(dz).start()
    for k in range(1, nm):
        m_copy(k).start()
    pending = []
    for k, peer in enumerate(x_ids):
        copy = remote(mm_hbm, mass_buf.at[xi], mm_s.at[k], mm_r.at[k], peer)
        copy.start()
        pending.append(copy)
    mass_copies = list(pending)
    for copy in local:
        copy.wait()
    if cs > 1:
        c_copy(0).start()

    def shard_of(k):
        return plus(xi, xs - lax.div(k, ws), xs) * ws + plus(yi, ws - lax.rem(k, ws), ws)

    def rows_of(shard):
        return pl.ds(pl.multiple_of(shard * mb, mb), mb)

    def make_scaled(shard):
        high, mid, low = [
            lax.dot_general(men_buf[shard], part, LHS_T, preferred_element_type=F32)
            for part in split3(aff_ref[...])
        ]
        scaled_ref[rows_of(shard), :] = ((low + mid) + high).astype(BF16)

    make_scaled(xy_me)
    tile = math.gcd(mb, 256)
    fold = wb // 128 if wb % 128 == 0 else 1
    lanes = wb // fold
    rsum_ref[...] = jnp.zeros_like(rsum_ref)

    def fill(q, start, count):
        block = wom_buf[q]
        for part in range(count):
            at = pl.ds(pl.multiple_of(start + part * tile, tile), tile)
            surplus = jnp.dot(scaled_ref[at, :], block, preferred_element_type=F32)
            kernel = jnp.exp(surplus - log_count)
            e_ref[q, at, :] = kernel.astype(BF16)
            total = rsum_ref[at, :]
            for piece in range(fold):
                total = total + kernel[:, piece * lanes:(piece + 1) * lanes]
            rsum_ref[at, :] = total

    def z_block(dz):
        return ci * zs + plus(zi, zs - dz, zs)

    fill(zc_me, xy_me * mb, mb // tile)

    def own_men(dz, carry):
        z_copy(dz).wait_recv()
        if cs > 1:
            c_copy(dz).start()
        fill(z_block(dz), xy_me * mb, mb // tile)
        return carry

    def other_men(k, carry):
        m_copy(k).wait_recv()
        shard = shard_of(k)
        make_scaled(shard)
        for z in range(zs):
            fill(ci * zs + z, shard * mb, mb // tile)
        return carry

    def other_core(dz, carry):
        c_copy(dz).wait_recv()
        fill(plus(ci, 1, cs) * zs + plus(zi, zs - dz, zs), 0, group_rows // tile)
        return carry

    lax.fori_loop(1, zs, own_men, 0)
    lax.fori_loop(1, nm, other_men, 0)
    if cs > 1:
        lax.fori_loop(0, zs, other_core, 0)

    def group_sum(value, buf, me, send, recv, peers):
        if not peers:
            return value
        buf[me] = value
        copies = []
        for k, peer in enumerate(peers):
            copy = remote(buf.at[me], buf.at[me], send.at[k], recv.at[k], peer)
            copy.start()
            copies.append(copy)
        for copy in copies:
            copy.wait_recv()
        pending.extend(copies)
        total = buf[0]
        for slot in range(1, buf.shape[0]):
            total = total + buf[slot]
        return total

    for copy in mass_copies:
        copy.wait_recv()
    men_mass = jnp.concatenate([mass_buf[x] for x in range(xs)], axis=1)
    men_full = jnp.concatenate([men_buf[k] for k in range(nm)], axis=1)
    mass_q = None
    for x in range(xs):
        order = [(z * xs + x) * cs + c for c in range(cs) for z in range(zs)]
        mine = jnp.concatenate([wm_ref[:, p * wb:(p + 1) * wb] for p in order], axis=0)
        mass_q = mine if mass_q is None else jnp.where(xi == x, mine, mass_q)

    def men_update(it, row_sum):
        return men_mass / group_sum(row_sum, r_buf.at[it], xy_me, rx_s.at[it], rx_r.at[it], xy_ids)

    def women_update(it, partial):
        return mass_q / group_sum(partial, c_buf.at[it], zc_me, cz_s.at[it], cz_r.at[it], zc_ids)

    zeros13 = jnp.zeros((13, group_rows), BF16)
    zeros13w = jnp.zeros((13, wb), BF16)

    def sweep(step, carry):
        for q in range(nb):
            carry = step(q, carry)
        return carry

    sums = rsum_ref[...]
    high = sums.astype(BF16)
    low = (sums - high.astype(F32)).astype(BF16)
    total = lax.dot_general(jnp.ones((16, 2 * lanes), BF16), jnp.concatenate([high, low], axis=1),
                            RHS_T, preferred_element_type=F32)
    scale = men_update(0, total[0:1])
    left0 = jnp.concatenate(list(split3(scale)) + [zeros13], axis=0)

    def col_step(q, carry):
        out = jnp.dot(left0, e_ref[q], preferred_element_type=F32)
        col_ref[q:q + 1, :] = out[0:1] + out[1:2] + out[2:3]
        return carry

    sweep(col_step, 0)
    col_ref[...] = women_update(0, col_ref[...])

    def row_step(q, total):
        lines = jnp.concatenate(list(split3(col_ref[q:q + 1, :])) + [zeros13w], axis=0)
        return total + lax.dot_general(lines, e_ref[q], RHS_T, preferred_element_type=F32)

    total = sweep(row_step, jnp.zeros((16, group_rows), F32))
    scale = men_update(1, total[0:1] + total[1:2] + total[2:3])
    for x in range(xs):
        scale_ref[x] = scale[:, x * rows:(x + 1) * rows]
    ms_out[...] = scale_ref[xi]

    weighted = (men_full.astype(F32) * scale).astype(BF16)
    left = jnp.concatenate([weighted] + list(split3(scale)) + [zeros13], axis=0)

    def both_step(q, carry):
        out = jnp.dot(left, e_ref[q], preferred_element_type=F32)
        t_ref[q] = out[0:traits]
        col_ref[q:q + 1, :] = (out[traits:traits + 1] + out[traits + 1:traits + 2]
                               + out[traits + 2:traits + 3])
        return carry

    sweep(both_step, 0)
    women_scale = women_update(1, col_ref[...])
    col_ref[...] = women_scale
    wx_buf[xi] = women_scale
    wx_copies = []
    for k, peer in enumerate(x_ids):
        copy = remote(wx_buf.at[xi], wx_buf.at[xi], wx_s.at[k], wx_r.at[k], peer)
        copy.start()
        wx_copies.append(copy)
    pending.extend(wx_copies)

    def moment_step(q, moment):
        inner = t_ref[q] * col_ref[q:q + 1, :]
        high = inner.astype(BF16)
        low = (inner - high.astype(F32)).astype(BF16)
        both = jnp.concatenate([high, low], axis=0)
        return moment + lax.dot_general(both, wom_buf[q], RHS_T, preferred_element_type=F32)

    moment = sweep(moment_step, jnp.zeros((2 * traits, traits), F32))
    moment = moment[0:traits] + moment[traits:]
    half = traits // 2
    packed = jnp.concatenate([moment[0:half], moment[half:]], axis=1)
    packed = group_sum(packed, mxy_buf, xy_me, rx_s.at[2], rx_r.at[2], xy_ids)
    packed = group_sum(packed, mc_buf, ci, mc_s, mc_r, c_ids)
    for copy in wx_copies:
        copy.wait_recv()
    for x in range(xs):
        scales = wx_buf[x]
        for q in range(nb):
            p = ((q % zs) * xs + x) * cs + q // zs
            ws_out[:, p * wb:(p + 1) * wb] = scales[q:q + 1, :]
    packed = group_sum(packed, mz_buf, zi, mz_s, mz_r, z_ids)
    moment = jnp.concatenate([packed[:, 0:traits], packed[:, traits:]], axis=0)
    up_out[...] = aff_ref[...] + obs_ref[...] - moment * (1.0 / men_total)

    for copy in pending:
        copy.wait_send()
    for dz in range(1, zs):
        z_copy(dz).wait_send()
    for k in range(1, nm):
        m_copy(k).wait_send()
    if cs > 1:
        for dz in range(zs):
            c_copy(dz).wait_send()


def solution(mesh):
    men_axis, women_axis = mesh.shape["men"], mesh.shape["women"]
    dims = factors(men_axis)
    zs, xs, cs = dims

    def on_device(men_traits, women_traits, affinity, observed, men_mass, women_mass):
        traits, mb = men_traits.shape
        wb = women_traits.shape[1]
        rows, cols = men_mass.shape[0], women_mass.shape[0]
        nm, nb = xs * women_axis, zs * cs
        dma = pltpu.SemaphoreType.DMA
        vmem = pl.BlockSpec(memory_space=pltpu.VMEM)
        anywhere = pl.BlockSpec(memory_space=pl.ANY)
        packed = (traits // 2, 2 * traits)
        out = pl.pallas_call(
            functools.partial(body, dims, women_axis, rows * men_axis, cols * women_axis),
            out_shape=(
                jax.ShapeDtypeStruct((1, rows), F32),
                jax.ShapeDtypeStruct((1, cols), F32),
                jax.ShapeDtypeStruct((traits, traits), F32),
            ),
            in_specs=[anywhere] * 6,
            out_specs=(vmem, vmem, vmem),
            scratch_shapes=[
                pltpu.VMEM((nm, traits, mb), BF16),
                pltpu.VMEM((nb, traits, wb), BF16),
                pltpu.VMEM((nm * mb, traits), BF16),
                pltpu.VMEM((nb, nm * mb, wb), BF16),
                pltpu.VMEM((nb, traits, wb), F32),
                pltpu.VMEM((nb, wb), F32),
                pltpu.VMEM((nm * mb, wb if wb % 128 else 128), F32),
                pltpu.VMEM((xs, 1, rows), F32),
                pltpu.VMEM((traits, traits), F32),
                pltpu.VMEM((traits, traits), F32),
                pltpu.VMEM((1, cols), F32),
                pltpu.VMEM((xs, 1, rows), F32),
                pltpu.VMEM((xs, nb, wb), F32),
                pltpu.VMEM((2, nm, 1, nm * mb), F32),
                pltpu.VMEM((2, nb, nb, wb), F32),
                pltpu.VMEM((nm,) + packed, F32),
                pltpu.VMEM((cs,) + packed, F32),
                pltpu.VMEM((zs,) + packed, F32),
                dma((6,)),
                dma((nm,)), dma((nm,)),
                dma((zs,)), dma((zs,)),
                dma((zs,)), dma((zs,)),
                dma((xs,)), dma((xs,)),
                dma((xs,)), dma((xs,)),
                dma((3, nm)), dma((3, nm)),
                dma((2, nb)), dma((2, nb)),
                dma((cs,)), dma((cs,)),
                dma((zs,)), dma((zs,)),
            ],
            compiler_params=pltpu.CompilerParams(
                collective_id=0, has_side_effects=True, vmem_limit_bytes=60 * 1024 * 1024),
        )(men_traits, women_traits, affinity, observed,
          men_mass.reshape(1, rows), women_mass.reshape(1, cols))
        return out[0].reshape(rows), out[1].reshape(cols), out[2]

    placed = (P(None, ("men", "women")), P(None, ("women", "men")), P(), P(), P("men"), P("women"))
    return jax.shard_map(
        on_device,
        mesh=mesh,
        in_specs=placed,
        out_specs=(P("men"), P("women"), P()),
        check_vma=False,
    )
```

time: 57.5 us -> 48.5 us (0.84)
  Pallas kernels: 53.3 us -> 44.4 us
    pallas_call x1, Pallas kernels: 53.3 us -> 44.4 us  [on_device(): pl.pallas_call(functools.partial(body, dims, women_axis, rows * men_axis,...]
where the time goes in v1:
time: 48.5 us; the launch traced here: 48.2 us
  Pallas kernels  44.4 us (92%)
  local copies, waits for them, and re-layouts  3.22 us (7%)
  between operations  0.65 us (1%)
    pallas_call x1, Pallas kernels, on_device(): pl.pallas_call(functools.partial(body, dims, women_axis, rows * men_axis,...  44.4 us
    unnamed x5, local copies, waits for them, and re-layouts  3.22 us

profile of v1, /device:TPU:0, one launch (start us, length us, event | category | flops | bytes accessed | tf_op | source)
XLA Modules:
  0.0 48.2 jit_solution(10509053105829647735)
XLA Ops:
  0.6 44.4 %shard_map.85 = (f32[1,1024]{1,0:T(1,128)}, f32[1,4096]{1,0:T(1,128)}, f32[64,64]{1,0:T(8,128)}) custom-call(bf16[64,512]{1,0:T(8,128)(2,1)} %men_ref.1, bf16[64,256]{1,0:T(8,128)(2,1)} %women_ref.1, f32[64,64]{1,0:T(8,128)} %aff_hbm.1, f32[64,64]{1,0:T(8,128)} %obs_hbm.1, f32[1,1024]{1,0:T(1,128)} %bitcast.6, f32[1,4096]{1,0:T(1,128)} %bitcast.4), custom_call_target="tpu_custom_call" | custom-call | tf_op jit(solution)/shard_map/pallas_call | solution.py:314
  45.0 0.0 copy-start
  45.0 1.3 %copy.12 = f32[1024]{0:T(1024)} copy(f32[1024]{0:T(1024)} %bitcast.7) | data formatting | bytes 8192
  46.3 1.3 %copy.13 = f32[4096]{0:T(1024)} copy(f32[4096]{0:T(1024)} %bitcast.5) | data formatting | bytes 32768
  47.6 0.0 copy-done
  47.6 0.6 %copy.14 = f32[64,64]{1,0:T(8,128)} copy(f32[64,64]{1,0:T(8,128)S(1)} %copy-done) | data formatting | bytes 32768
Async XLA Ops:
  45.0 2.6 %copy-start = (f32[64,64]{1,0:T(8,128)S(1)}, f32[64,64]{1,0:T(8,128)}, u32[]{:S(2)}) copy-start(f32[64,64]{1,0:T(8,128)} %get-tuple-element.14) | copy-start | bytes 49156
